TPU v7x, 256 devices: a whole 4x4x8 slice. The times are simulated.
256 devices in a mesh: req: 4 (over x), exp: 64 (over z, y, core).
Axes of the slice: x: 4, y: 4, z: 8, core: 2. Of those that a mesh axis runs over, the one named last changes fastest.
Arguments:
- hidden: bfloat16 [256, 32, 2048], P(('req', 'exp')), may hold values from -6 to 6
- queries: bfloat16 [256, 32, 3072], P(('req', 'exp'))
- new_latent: bfloat16 [256, 32, 576], P(('req', 'exp')), may hold values from -6 to 6
- pages: bfloat16 [2048, 128, 576], P(('req', 'exp'))
- page_table: int32 [256, 8], P(('req', 'exp')), may hold values from 0 to 7, each once within a row
- cache_len: int32 [256], P(('req', 'exp')), may hold values from 1 to 992, as said below
- parents: int32 [256, 32], P(('req', 'exp')), may hold values from 0 to 30, as said below
- accept_path: int32 [256, 32], P(('req', 'exp')), may hold values from 0 to 31, as said below
- accept_count: int32 [256], P(('req', 'exp')), may hold values from 1 to 32, as said below
- key_up: bfloat16 [16, 128, 512], replicated, may hold values from -0.5 to 0.5
- value_up: bfloat16 [16, 512, 128], replicated, may hold values from -0.25 to 0.25
- out_proj: bfloat16 [2048, 2048], P(None, 'req'), may hold values from -0.125 to 0.125
- norm_gain: bfloat16 [2048], replicated, may hold values from 0.5 to 1.5
- route_ids: int32 [4, 64, 32, 6], P(None, 'exp'), may hold values from 0 to 63, all different within a row; in each aligned block of 32 rows (0 to 31, 32 to 63, ..., all dimensions but the last counted through in order) at most 6 rows name the same one
- route_weights: float32 [4, 64, 32, 6], P(None, 'exp'), may hold values from 0.2 to 1.2
- w_gate: bfloat16 [64, 2048, 1408], P('exp', None, 'req'), may hold values from -0.125 to 0.125
- w_up: bfloat16 [64, 2048, 1408], P('exp', None, 'req'), may hold values from -0.125 to 0.125
- w_down: bfloat16 [64, 1408, 2048], P('exp', 'req'), may hold values from -0.15625 to 0.15625
Outputs:
- layer_out: bfloat16 [256, 32, 2048], P(('req', 'exp'))
- new_pages: bfloat16 [2048, 128, 576], P(('req', 'exp'))
Inputs may be any that keep to these rules, and one draw needn't show every extreme that they name: `route_ids`: in each request no expert is named by more than 6 tokens, a bound that some block reaches. `page_table`: each row is an order of the 8 pages of the request's pool. `cache_len`: some request holds the largest length. parents[q, 0] = 0; for t >= 1 the parent of t is below t; one request's tree is a single chain. `accept_path`: entry k for k < accept_count is the ancestor at depth k of the last accepted token, entry 0 the root; later entries are 0. `accept_count`: one more than the depth of the last accepted token.
All inputs are finite; a program needn't handle non-finite values.
Results may differ from a plain program's by a relative error of at most 0.023.
Values may be sent and summed in bfloat16 or wider, within the bound.
A program may use at most 128 MiB of HBM per device.

v0:
```python
import math
import jax
import jax.numpy as jnp
from jax import lax
from jax.sharding import PartitionSpec as P

TOP = 6
TREE = 32


def ancestry(parent_row):
    count = parent_row.shape[0]
    ident = jnp.eye(count, dtype=jnp.int32)
    linked = (parent_row[:, None] == jnp.arange(count, dtype=jnp.int32)[None, :]).astype(jnp.int32)
    reach = jnp.minimum(ident + linked, 1)
    for sweep in range(count.bit_length()):
        reach = jnp.minimum(jnp.dot(reach, reach), 1)
    return reach


def attend(query_row, page_pool, table_row, length, parent_row, fresh, key_up, value_up):
    count = query_row.shape[0]
    heads = key_up.shape[0]
    nope = key_up.shape[1]
    latent = key_up.shape[2]
    shaped = query_row.reshape(count, heads, -1)
    scale = 1.0 / math.sqrt(shaped.shape[2])
    q_nope = shaped[:, :, :nope]
    q_rope = shaped[:, :, nope:]
    q_latent = jnp.einsum(
        "thn,hnc->thc", q_nope, key_up, preferred_element_type=jnp.float32
    ).astype(jnp.bfloat16)
    q_full = jnp.concatenate([q_latent, q_rope], axis=2)
    cache_rows = jnp.take(page_pool, table_row, axis=0).reshape(-1, page_pool.shape[2])
    score_cache = (
        jnp.einsum("thc,kc->thk", q_full, cache_rows, preferred_element_type=jnp.float32) * scale
    )
    score_tree = (
        jnp.einsum("thc,jc->thj", q_full, fresh, preferred_element_type=jnp.float32) * scale
    )
    live = jnp.arange(cache_rows.shape[0], dtype=jnp.int32) < length
    score_cache = jnp.where(live[None, None, :], score_cache, -1e30)
    score_tree = jnp.where(ancestry(parent_row)[:, None, :] > 0, score_tree, -1e30)
    peak = jnp.maximum(jnp.max(score_cache, axis=2), jnp.max(score_tree, axis=2))[:, :, None]
    exp_cache = jnp.exp(score_cache - peak)
    exp_tree = jnp.exp(score_tree - peak)
    total = jnp.sum(exp_cache, axis=2, keepdims=True) + jnp.sum(exp_tree, axis=2, keepdims=True)
    prob_cache = (exp_cache / total).astype(jnp.bfloat16)
    prob_tree = (exp_tree / total).astype(jnp.bfloat16)
    context = jnp.einsum(
        "thk,kc->thc", prob_cache, cache_rows[:, :latent], preferred_element_type=jnp.float32
    )
    context = context + jnp.einsum(
        "thj,jc->thc", prob_tree, fresh[:, :latent], preferred_element_type=jnp.float32
    )
    context = context.astype(jnp.bfloat16)
    head_out = jnp.einsum(
        "thc,hcv->thv", context, value_up, preferred_element_type=jnp.float32
    ).astype(jnp.bfloat16)
    return head_out.reshape(count, -1)


def write_rows(page_pool, table_row, length, path_row, count, fresh):
    pool_len = page_pool.shape[0]
    page_size = page_pool.shape[1]
    pool_ids = jnp.arange(pool_len, dtype=jnp.int32)
    match = table_row[None, :] == pool_ids[:, None]
    logical = jnp.sum(jnp.where(match, pool_ids[None, :], 0), axis=1)
    position = logical[:, None] * page_size + jnp.arange(page_size, dtype=jnp.int32)[None, :]
    offset = position - length
    valid = (offset >= 0) & (offset < count)
    source = jnp.take(path_row, jnp.clip(offset, 0, path_row.shape[0] - 1))
    written = jnp.take(fresh, source, axis=0)
    return jnp.where(valid[:, :, None], written, page_pool)


def slot_tables(route_rows, weight_rows, experts, capacity):
    expert_ids = jnp.arange(experts, dtype=jnp.int32)
    hits = route_rows[:, :, :, None] == expert_ids
    chosen = jnp.sum(hits.astype(jnp.int32), axis=2)
    weight_by = jnp.sum(jnp.where(hits, weight_rows[:, :, :, None], 0.0), axis=2)
    before = jnp.cumsum(chosen, axis=1) - chosen
    chosen_t = jnp.transpose(chosen, (0, 2, 1))
    before_t = jnp.transpose(before, (0, 2, 1))
    weight_t = jnp.transpose(weight_by, (0, 2, 1))
    slot_ids = jnp.arange(capacity, dtype=jnp.int32)
    placed = (chosen_t[:, :, None, :] > 0) & (
        before_t[:, :, None, :] == slot_ids[None, None, :, None]
    )
    weighted = jnp.where(placed, weight_t[:, :, None, :], 0.0)
    return (placed.astype(jnp.bfloat16), weighted)


def local(
    hidden,
    queries,
    new_latent,
    pages,
    page_table,
    cache_len,
    parents,
    accept_path,
    accept_count,
    key_up,
    value_up,
    out_proj,
    norm_gain,
    route_ids,
    route_weights,
    w_gate,
    w_up,
    w_down,
):
    width = hidden.shape[2]
    head_out = attend(
        queries[0], pages, page_table[0], cache_len[0], parents[0], new_latent[0], key_up, value_up
    )
    column_block = jnp.dot(
        lax.all_gather(head_out, "req", axis=0, tiled=True),
        out_proj,
        preferred_element_type=jnp.float32,
    ).astype(jnp.bfloat16)
    projected = lax.all_to_all(column_block, "req", split_axis=0, concat_axis=1, tiled=True)
    mixed = (hidden[0].astype(jnp.float32) + projected.astype(jnp.float32)).astype(jnp.bfloat16)
    mixed_f = mixed.astype(jnp.float32)
    normed = (
        mixed_f
        * lax.rsqrt(jnp.mean(mixed_f * mixed_f, axis=1, keepdims=True) + 1e-06)
        * norm_gain.astype(jnp.float32)
    ).astype(jnp.bfloat16)
    experts = lax.axis_size("exp") * w_gate.shape[0]
    capacity = max(2, min(TREE, 2 * TREE * TOP // experts))
    gate_local = w_gate[0]
    up_local = w_up[0]
    down_local = w_down[0]
    copies = lax.all_gather(normed[None], "req", axis=0, tiled=True)
    placed, weighted = slot_tables(route_ids[:, 0], route_weights[:, 0], experts, capacity)
    outbound = jnp.einsum(
        "gxct,gtd->xgcd", placed, copies, preferred_element_type=jnp.float32
    ).astype(jnp.bfloat16)
    slot_block = lax.all_to_all(outbound, "exp", split_axis=0, concat_axis=0, tiled=True)
    flat = slot_block.reshape(-1, width)
    gate_val = jnp.dot(flat, gate_local, preferred_element_type=jnp.float32)
    up_val = jnp.dot(flat, up_local, preferred_element_type=jnp.float32)
    active = (jax.nn.silu(gate_val) * up_val).astype(jnp.bfloat16)
    returned = lax.all_to_all(
        jnp.dot(active, down_local, preferred_element_type=jnp.float32)
        .astype(jnp.bfloat16)
        .reshape(slot_block.shape),
        "exp",
        split_axis=0,
        concat_axis=0,
        tiled=True,
    )
    partial_value = jnp.einsum("gxct,xgcd->gtd", weighted, returned.astype(jnp.float32))
    moe = lax.psum_scatter(
        partial_value.astype(jnp.bfloat16), "req", scatter_dimension=0, tiled=True
    ).astype(jnp.float32)[0]
    layer_out = (mixed_f + moe).astype(jnp.bfloat16)[None]
    new_pool = write_rows(
        pages, page_table[0], cache_len[0], accept_path[0], accept_count[0], new_latent[0]
    )
    return (layer_out, new_pool)


def solution(mesh):
    in_specs = (
        P(("req", "exp"), None, None),
        P(("req", "exp"), None, None),
        P(("req", "exp"), None, None),
        P(("req", "exp"), None, None),
        P(("req", "exp"), None),
        P(("req", "exp")),
        P(("req", "exp"), None),
        P(("req", "exp"), None),
        P(("req", "exp")),
        P(),
        P(),
        P(None, "req"),
        P(),
        P(None, "exp", None, None),
        P(None, "exp", None, None),
        P("exp", None, "req"),
        P("exp", None, "req"),
        P("exp", "req", None),
    )
    out_specs = (P(("req", "exp"), None, None), P(("req", "exp"), None, None))
    return jax.shard_map(local, mesh=mesh, in_specs=in_specs, out_specs=out_specs, check_vma=False)
```

profile of v0, /device:TPU:8, one launch (start us, length us, event | category | flops | bytes accessed | tf_op | source)
XLA Modules:
  0.0 495.9 jit_solution(1943214140383278034)
XLA Ops:
  7.2 1.4 reshape_squeeze.3
  8.6 0.7 slice.22
  9.3 0.7 fusion.78
  10.0 0.7 compare_and_fusion.1
  11.4 1.7 gather_fusion
  13.1 2.4 copy.166
  15.6 0.4 fusion.18
  16.0 0.8 copy-done.6
  16.9 0.3 bitcast_select_fusion
  17.3 2.4 fusion.9
  19.7 0.4 convolution_minimum_fusion.4
  20.2 0.3 convolution_minimum_fusion.2
  20.5 0.3 fusion.23
  21.0 0.7 fusion.85
  21.8 2.1 fusion.10
  24.2 2.1 divide_convert_fusion
  26.3 1.8 fusion.24
  28.1 2.5 fusion.22
  30.6 13.1 %all_gather.6 = bf16[128,2048]{1,0:T(8,128)(2,1)S(1)} all-gather(bf16[32,2048]{1,0:T(8,128)(2,1)S(1)} %bitcast.125), channel_id=1, replica_groups=mesh['req'=4,'exp'=64] {'req'}, dimensions={0}, use_global_device_ids=true | all-gather | bytes 655360 | tf_op jit(solution)/shard_map/all_gather | solution.py:119
  43.8 2.7 convolution_convert_fusion.2
  46.5 4.4 all-to-all-start
  50.9 0.2 convert_reduce_fusion
  51.2 5.6 %all-to-all-done = bf16[4,32,512]{2,1,0:T(8,128)(2,1)S(1)} async-done(((bf16[4,32,512]{2,1,0:T(8,128)(2,1)}), bf16[4,32,512]{2,1,0:T(8,128)(2,1)S(1)}, u32[]{:S(2)}, u32[]{:S(2)}) %all-to-all-start) | async-done | bytes 131104 | tf_op jit(solution)/shard_map/all_to_all | solution.py:123
  56.9 0.2 copy.151
  57.1 0.2 reshape.259
  57.4 0.1 multiply_reduce_fusion
  57.6 13.7 %all_gather.7 = bf16[4,32,2048]{2,1,0:T(8,128)(2,1)S(1)} all-gather(bf16[1,32,2048]{2,1,0:T(8,128)(2,1)S(1)} %fusion.38), channel_id=1, replica_groups=mesh['req'=4,'exp'=64] {'req'}, dimensions={0}, use_global_device_ids=true | all-gather | bytes 655360 | tf_op jit(solution)/shard_map/all_gather | solution.py:136
  71.3 4.5 convert_bitcast_fusion
  75.8 10.3 %copy.157 = bf16[64,4,6,2048]{3,1,2,0:T(4,128)(2,1)} copy(bf16[64,4,6,2048]{3,0,2,1:T(8,128)(2,1)} %convert_bitcast_fusion) | data formatting | bytes 12582912 | tf_op jit(solution)/shard_map/convert_element_type | solution.py:140
  86.1 153.4 %all_to_all.23 = bf16[64,4,6,2048]{3,1,2,0:T(4,128)(2,1)S(1)} all-to-all(bf16[64,4,6,2048]{3,1,2,0:T(4,128)(2,1)} %copy.157), channel_id=1, replica_groups=mesh['req'=4,'exp'=64] {'exp'}, dimensions={0} | all-to-all | bytes 12582912 | tf_op jit(solution)/shard_map/all_to_all | solution.py:141
  239.5 10.7 %copy.158 = bf16[64,4,6,2048]{3,2,1,0:T(8,128)(2,1)} copy(bf16[64,4,6,2048]{3,1,2,0:T(4,128)(2,1)S(1)} %all_to_all.23) | data formatting | bytes 12582912 | tf_op jit(solution)/shard_map/all_to_all | solution.py:141
  250.2 11.1 %reshape.257 = bf16[1536,2048]{1,0:T(8,128)(2,1)} reshape(bf16[64,4,6,2048]{3,2,1,0:T(8,128)(2,1)} %copy.158) | data formatting | bytes 12582912 | tf_op jit(solution)/shard_map/reshape | solution.py:142
  261.3 7.0 %fusion.13 = f32[1536,352]{0,1:T(8,128)} fusion(bf16[1536,2048]{1,0:T(8,128)(2,1)} %reshape.257, bf16[1,2048,352]{1,2,0:T(8,128)(2,1)} %param.33), kind=kOutput, calls=%fused_computation.18 | convolution fusion | flops 2214592512 | bytes 9895936 | tf_op jit(solution)/shard_map/dot_general | solution.py:143
  268.3 12.2 %convolution_convert_fusion = bf16[1536,2048]{1,0:T(8,128)(2,1)} fusion(bf16[1,352,2048]{2,1,0:T(8,128)(2,1)} %param.35, bf16[1536,2048]{1,0:T(8,128)(2,1)} %reshape.257, f32[1536,352]{0,1:T(8,128)} %fusion.13, bf16[1,2048,352]{1,2,0:T(8,128)(2,1)} %param.34), kind=kOutput, calls=%fused_computation.3 | convolution fusion | flops 4435574784 | bytes 17629184 | tf_op jit(solution)/shard_map/dot_general | solution.py:147
  280.4 11.4 %reshape.258 = bf16[64,4,6,2048]{3,2,1,0:T(8,128)(2,1)} reshape(bf16[1536,2048]{1,0:T(8,128)(2,1)} %convolution_convert_fusion) | data formatting | bytes 12582912 | tf_op jit(solution)/shard_map/reshape | solution.py:149
  291.8 18.8 %copy.159 = bf16[64,4,6,2048]{3,1,2,0:T(4,128)(2,1)} copy(bf16[64,4,6,2048]{3,2,1,0:T(8,128)(2,1)} %reshape.258) | data formatting | bytes 12582912 | tf_op jit(solution)/shard_map/reshape | solution.py:149
  310.7 5.7 %all-to-all-start.2 = ((bf16[64,4,6,2048]{3,1,2,0:T(4,128)(2,1)}), bf16[64,4,6,2048]{3,1,2,0:T(4,128)(2,1)}, u32[]{:S(2)}, u32[]{:S(2)}) async-start(bf16[64,4,6,2048]{3,1,2,0:T(4,128)(2,1)} %copy.159), calls=%async_computation.2 | async-start | bytes 12582912 | tf_op jit(solution)/shard_map/all_to_all | solution.py:146
  316.5 0.1 select_reduce_fusion.1
  316.6 0.3 select_reduce_fusion
  316.9 140.8 %all-to-all-done.2 = bf16[64,4,6,2048]{3,1,2,0:T(4,128)(2,1)} async-done(((bf16[64,4,6,2048]{3,1,2,0:T(4,128)(2,1)}), bf16[64,4,6,2048]{3,1,2,0:T(4,128)(2,1)}, u32[]{:S(2)}, u32[]{:S(2)}) %all-to-all-start.2) | async-done | bytes 6291488 | tf_op jit(solution)/shard_map/all_to_all | solution.py:146
  457.7 10.5 %fusion.6 = bf16[4,32,2048]{2,1,0:T(8,128)(2,1)} fusion(bf16[64,4,6,2048]{3,1,2,0:T(4,128)(2,1)} %all-to-all-done.2, bf16[4,64,32]{1,2,0:T(8,128)(2,1)S(1)} %bitcast.128, s32[4,64,32]{1,2,0:T(8,128)S(1)} %subtract_bitcast_fusion, pred[4,64,32]{1,2,0:T(8,128)(4,1)S(1)} %compare_bitcast_fusion), kind=kOutput, calls=%fused_computation.10 | convolution fusion | flops 201474048 | bytes 6873088 | tf_op jit(solution)/shard_map/gxct,xgcd->gtd/dot_general | solution.py:155
  468.3 0.5 copy-done.2
  468.8 6.6 %gather_fusion.1 = s32[1024]{0:T(1024)S(1)} fusion(s32[32]{0:T(128)S(1)} %bitcast.120, s32[1024]{0:T(1024)S(1)} %bitcast_clamp_fusion), kind=kCustom, calls=%fused_computation.1 | custom fusion | bytes 12288 | tf_op jit(solution)/shard_map/jit(_take)/gather | solution.py:72
  475.5 4.0 gather_fusion.2
  479.5 1.4 copy.161
  481.7 2.6 select_select_fusion
  484.3 2.9 reduce-scatter.2.cloned.1.call-done
  487.2 1.7 fusion.39
  (65 shorter events, 1.4 us)
Async XLA Ops:
  7.2 8.4 %copy-start = (bf16[16,128,512]{2,1,0:T(8,128)(2,1)S(1)}, bf16[16,128,512]{2,1,0:T(8,128)(2,1)}, u32[]{:S(2)}) copy-start(bf16[16,128,512]{2,1,0:T(8,128)(2,1)} %param.27) | copy-start | bytes 6291460
  7.2 4.2 copy-start.4
  11.3 4.7 copy-start.9
  11.4 4.2 copy-start.11
  15.5 1.4 copy-start.5
  16.0 0.8 copy-start.6
  17.2 2.5 copy-start.15
  17.2 3.7 copy-start.3
  17.2 3.7 copy-start.7
  17.2 3.7 copy-start.10
  30.6 20.3 %copy-start.12 = (s32[4,1,32,6]{2,1,3,0:T(1,128)S(1)}, s32[4,1,32,6]{2,1,3,0:T(1,128)}, u32[]{:S(2)}) copy-start(s32[4,1,32,6]{2,1,3,0:T(1,128)} %param.31) | copy-start | bytes 9220
  30.6 20.6 %copy-start.14 = (bf16[2048]{0:T(1024)(128)(2,1)S(1)}, bf16[2048]{0:T(1024)(128)(2,1)}, u32[]{:S(2)}) copy-start(bf16[2048]{0:T(1024)(128)(2,1)} %param.30) | copy-start | bytes 12292
  46.5 10.9 %copy-start.8 = (bf16[1,32,2048]{2,1,0:T(8,128)(2,1)S(1)}, bf16[1,32,2048]{2,1,0:T(8,128)(2,1)}, u32[]{:S(2)}) copy-start(bf16[1,32,2048]{2,1,0:T(8,128)(2,1)} %param.18) | copy-start | bytes 393220
  46.5 10.4 %all-to-all-start = ((bf16[4,32,512]{2,1,0:T(8,128)(2,1)}), bf16[4,32,512]{2,1,0:T(8,128)(2,1)S(1)}, u32[]{:S(2)}, u32[]{:S(2)}) async-start(bf16[4,32,512]{2,1,0:T(8,128)(2,1)} %bitcast.14), calls=%async_computation | async-start | bytes 262144 | tf_op jit(solution)/shard_map/all_to_all | solution.py:123
  310.7 5.8 %copy-start.13 = (f32[4,1,32,6]{2,1,3,0:T(1,128)S(1)}, f32[4,1,32,6]{2,1,3,0:T(1,128)}, u32[]{:S(2)}) copy-start(f32[4,1,32,6]{2,1,3,0:T(1,128)} %param.32) | copy-start | bytes 9220
  310.7 5.8 %copy-start.16 = (s32[1,8]{1,0:T(1,128)S(1)}, s32[1,8]{1,0:T(1,128)}, u32[]{:S(2)}) copy-start(s32[1,8]{1,0:T(1,128)} %param.22) | copy-start | bytes 100
  310.7 147.0 %all-to-all-start.2 = ((bf16[64,4,6,2048]{3,1,2,0:T(4,128)(2,1)}), bf16[64,4,6,2048]{3,1,2,0:T(4,128)(2,1)}, u32[]{:S(2)}, u32[]{:S(2)}) async-start(bf16[64,4,6,2048]{3,1,2,0:T(4,128)(2,1)} %copy.159), calls=%async_computation.2 | async-start | bytes 12582912 | tf_op jit(solution)/shard_map/all_to_all | solution.py:146
  316.4 170.8 %reduce-scatter.2.cloned.1.call-start = ((), (), s32[]{:S(2)}) async-start(), calls=%async_computation.4 | async-start | bytes 655360 | tf_op jit(solution)/shard_map/reduce_scatter | solution.py:156
  468.2 0.7 copy-start.2
  481.7 7.2 %copy-start.1 = (bf16[16,128,512]{2,1,0:T(8,128)(2,1)S(1)}, bf16[16,128,512]{2,1,0:T(8,128)(2,1)}, u32[]{:S(2)}) copy-start(bf16[16,128,512]{2,1,0:T(8,128)(2,1)} %param.27) | copy-start | bytes 6291460
Sparse Core Ops, SparseCore 0:
  468.3 18.8 reduce-scatter.1
where the time goes:
time: 503 us; the launch traced here: 496 us
  blocking collectives  180 us (36%)
  waiting for transfers between devices  149 us (30%)
  local copies, waits for them, and re-layouts  82.8 us (16%)
  matrix products  45.8 us (9%)
  between operations  16 us (3%)
  other arithmetic  11.5 us (2%)
  starting transfers between devices  10.2 us (2%)
    all_to_all x1, blocking collectives, local(): lax.all_to_all(outbound, 'exp', split_axis=0, concat_axis=0, tiled=True)  153 us
    all_to_all x1, waiting for transfers between devices, local(): lax.all_to_all(jnp.dot(active, down_local, preferred_element_type=jnp.flo...  141 us
    reshape x2, local copies, waits for them, and re-layouts, local(): returned = lax.all_to_all(jnp.dot(active, down_local, preferred_element_t...  30.2 us
    all_gather x1, blocking collectives, local(): copies = lax.all_gather(normed[None], 'req', axis=0, tiled=True)  13.7 us
    all_gather x1, blocking collectives, local(): lax.all_gather(head_out, 'req', axis=0, tiled=True)  13.1 us
    dot_general x1, matrix products, local(): jnp.dot(active, down_local, preferred_element_type=jnp.float32)  12.2 us
    reshape x1, local copies, waits for them, and re-layouts, local(): flat = slot_block.reshape(-1, width)  11.1 us
    all_to_all x1, local copies, waits for them, and re-layouts, local(): lax.all_to_all(outbound, 'exp', split_axis=0, concat_axis=0, tiled=True)  10.7 us
  transfers between devices with their start and end apart: 3, of which 3 were waited for; matrix products, arithmetic and copies ran while one was open for 3% of the time, Pallas kernels for 0%

commit v1 on v0

--- a/solution.py
+++ b/solution.py
@@ -6,6 +6,12 @@
 
 TOP = 6
 TREE = 32
+
+
+def gather_by_exchange(x, axis, dim):
+    count = lax.axis_size(axis)
+    repeats = [count if d == dim else 1 for d in range(x.ndim)]
+    return lax.all_to_all(jnp.tile(x, repeats), axis, split_axis=dim, concat_axis=dim, tiled=True)
 
 
 def ancestry(parent_row):
@@ -116,9 +122,7 @@
         queries[0], pages, page_table[0], cache_len[0], parents[0], new_latent[0], key_up, value_up
     )
     column_block = jnp.dot(
-        lax.all_gather(head_out, "req", axis=0, tiled=True),
-        out_proj,
-        preferred_element_type=jnp.float32,
+        gather_by_exchange(head_out, "req", 0), out_proj, preferred_element_type=jnp.float32
     ).astype(jnp.bfloat16)
     projected = lax.all_to_all(column_block, "req", split_axis=0, concat_axis=1, tiled=True)
     mixed = (hidden[0].astype(jnp.float32) + projected.astype(jnp.float32)).astype(jnp.bfloat16)

time: 503 us -> 503 us (level)
  blocking collectives: 180 us -> 166 us
  waiting for transfers between devices: 149 us -> 159 us
    all_gather x1 -> x0, blocking collectives: 13.1 us -> none  [local(): lax.all_gather(head_out, 'req', axis=0, tiled=True)]
    all_to_all x0 -> x1, waiting for transfers between devices: none -> 9.18 us  [gather_by_exchange(): lax.all_to_all(jnp.tile(x, repeats), axis, split_axis=dim, concat_axis=di...]
  transfers between devices with their start and end apart: 3 -> 4, of which waited for: 3 -> 4; matrix products, arithmetic and copies ran while one was open for 3% -> 3% of each run, Pallas kernels for 0% -> 0%
where the time goes in v1:
time: 503 us; the launch traced here: 496 us
  blocking collectives  166 us (33%)
  waiting for transfers between devices  159 us (32%)
  local copies, waits for them, and re-layouts  83.7 us (17%)
  matrix products  45.8 us (9%)
  between operations  16 us (3%)
  starting transfers between devices  13.6 us (3%)
  other arithmetic  11.5 us (2%)
    all_to_all x1, blocking collectives, local(): lax.all_to_all(outbound, 'exp', split_axis=0, concat_axis=0, tiled=True)  153 us
    all_to_all x1, waiting for transfers between devices, local(): lax.all_to_all(jnp.dot(active, down_local, preferred_element_type=jnp.flo...  141 us
    reshape x2, local copies, waits for them, and re-layouts, local(): returned = lax.all_to_all(jnp.dot(active, down_local, preferred_element_t...  30.2 us
    all_gather x1, blocking collectives, local(): copies = lax.all_gather(normed[None], 'req', axis=0, tiled=True)  13 us
    dot_general x1, matrix products, local(): jnp.dot(active, down_local, preferred_element_type=jnp.float32)  12.2 us
    reshape x1, local copies, waits for them, and re-layouts, local(): flat = slot_block.reshape(-1, width)  11 us
    all_to_all x1, local copies, waits for them, and re-layouts, local(): lax.all_to_all(outbound, 'exp', split_axis=0, concat_axis=0, tiled=True)  10.7 us
    dot_general x1, matrix products, local(): jnp.einsum('gxct,xgcd->gtd', weighted, returned.astype(jnp.float32))  10.5 us
  transfers between devices with their start and end apart: 4, of which 4 were waited for; matrix products, arithmetic and copies ran while one was open for 3% of the time, Pallas kernels for 0%

profile of v1, /device:TPU:8, one launch (start us, length us, event | category | flops | bytes accessed | tf_op | source)
XLA Modules:
  0.0 495.8 jit_solution(13725520204014004182)
XLA Ops:
  7.2 1.4 reshape_squeeze.3
  8.6 0.7 slice.22
  9.3 0.7 fusion.78
  10.0 0.7 compare_and_fusion.1
  11.4 1.7 gather_fusion
  13.1 2.4 copy.166
  15.6 0.4 fusion.18
  16.0 0.8 copy-done.6
  16.9 0.3 bitcast_select_fusion
  17.3 2.4 fusion.9
  19.7 0.4 convolution_minimum_fusion.4
  20.2 0.3 convolution_minimum_fusion.2
  20.5 0.3 fusion.23
  21.0 0.7 fusion.85
  21.8 2.1 fusion.10
  24.2 2.1 divide_convert_fusion
  26.3 1.8 fusion.24
  28.1 2.5 fusion.22
  30.6 0.8 tile.9
  31.5 4.4 all-to-all-start
  35.9 0.2 convert_reduce_fusion
  36.2 9.2 %all-to-all-done = bf16[4,32,2048]{2,1,0:T(8,128)(2,1)S(1)} async-done(((bf16[4,32,2048]{2,1,0:T(8,128)(2,1)}), bf16[4,32,2048]{2,1,0:T(8,128)(2,1)S(1)}, u32[]{:S(2)}, u32[]{:S(2)}) %all-to-all-start) | async-done | bytes 524320 | tf_op jit(solution)/shard_map/all_to_all | solution.py:14
  45.4 2.7 convolution_convert_fusion.2
  48.1 3.3 all-to-all-start.1
  51.5 5.9 %all-to-all-done.1 = bf16[4,32,512]{2,1,0:T(8,128)(2,1)S(1)} async-done(((bf16[4,32,512]{2,1,0:T(8,128)(2,1)}), bf16[4,32,512]{2,1,0:T(8,128)(2,1)S(1)}, u32[]{:S(2)}, u32[]{:S(2)}) %all-to-all-start.1) | async-done | bytes 131104 | tf_op jit(solution)/shard_map/all_to_all | solution.py:127
  57.4 0.2 copy.151
  57.6 0.2 reshape.262
  58.1 13.0 %all_gather.3 = bf16[4,32,2048]{2,1,0:T(8,128)(2,1)S(1)} all-gather(bf16[1,32,2048]{2,1,0:T(8,128)(2,1)S(1)} %fusion.38), channel_id=1, replica_groups=mesh['req'=4,'exp'=64] {'req'}, dimensions={0}, use_global_device_ids=true | all-gather | bytes 655360 | tf_op jit(solution)/shard_map/all_gather | solution.py:140
  71.1 4.5 convert_bitcast_fusion
  75.6 10.3 %copy.157 = bf16[64,4,6,2048]{3,1,2,0:T(4,128)(2,1)} copy(bf16[64,4,6,2048]{3,0,2,1:T(8,128)(2,1)} %convert_bitcast_fusion) | data formatting | bytes 12582912 | tf_op jit(solution)/shard_map/convert_element_type | solution.py:144
  85.9 153.5 %all_to_all.32 = bf16[64,4,6,2048]{3,1,2,0:T(4,128)(2,1)S(1)} all-to-all(bf16[64,4,6,2048]{3,1,2,0:T(4,128)(2,1)} %copy.157), channel_id=1, replica_groups=mesh['req'=4,'exp'=64] {'exp'}, dimensions={0} | all-to-all | bytes 12582912 | tf_op jit(solution)/shard_map/all_to_all | solution.py:145
  239.3 10.7 %copy.158 = bf16[64,4,6,2048]{3,2,1,0:T(8,128)(2,1)} copy(bf16[64,4,6,2048]{3,1,2,0:T(4,128)(2,1)S(1)} %all_to_all.32) | data formatting | bytes 12582912 | tf_op jit(solution)/shard_map/all_to_all | solution.py:145
  250.1 11.0 %reshape.260 = bf16[1536,2048]{1,0:T(8,128)(2,1)} reshape(bf16[64,4,6,2048]{3,2,1,0:T(8,128)(2,1)} %copy.158) | data formatting | bytes 12582912 | tf_op jit(solution)/shard_map/reshape | solution.py:146
  261.1 7.0 %fusion.13 = f32[1536,352]{0,1:T(8,128)} fusion(bf16[1536,2048]{1,0:T(8,128)(2,1)} %reshape.260, bf16[1,2048,352]{1,2,0:T(8,128)(2,1)} %param.33), kind=kOutput, calls=%fused_computation.18 | convolution fusion | flops 2214592512 | bytes 9895936 | tf_op jit(solution)/shard_map/dot_general | solution.py:147
  268.1 12.2 %convolution_convert_fusion = bf16[1536,2048]{1,0:T(8,128)(2,1)} fusion(bf16[1,352,2048]{2,1,0:T(8,128)(2,1)} %param.35, bf16[1536,2048]{1,0:T(8,128)(2,1)} %reshape.260, f32[1536,352]{0,1:T(8,128)} %fusion.13, bf16[1,2048,352]{1,2,0:T(8,128)(2,1)} %param.34), kind=kOutput, calls=%fused_computation.3 | convolution fusion | flops 4435574784 | bytes 17629184 | tf_op jit(solution)/shard_map/dot_general | solution.py:151
  280.2 11.4 %reshape.261 = bf16[64,4,6,2048]{3,2,1,0:T(8,128)(2,1)} reshape(bf16[1536,2048]{1,0:T(8,128)(2,1)} %convolution_convert_fusion) | data formatting | bytes 12582912 | tf_op jit(solution)/shard_map/reshape | solution.py:153
  291.7 18.8 %copy.159 = bf16[64,4,6,2048]{3,1,2,0:T(4,128)(2,1)} copy(bf16[64,4,6,2048]{3,2,1,0:T(8,128)(2,1)} %reshape.261) | data formatting | bytes 12582912 | tf_op jit(solution)/shard_map/reshape | solution.py:153
  310.5 5.8 %all-to-all-start.3 = ((bf16[64,4,6,2048]{3,1,2,0:T(4,128)(2,1)}), bf16[64,4,6,2048]{3,1,2,0:T(4,128)(2,1)}, u32[]{:S(2)}, u32[]{:S(2)}) async-start(bf16[64,4,6,2048]{3,1,2,0:T(4,128)(2,1)} %copy.159), calls=%async_computation.3 | async-start | bytes 12582912 | tf_op jit(solution)/shard_map/all_to_all | solution.py:150
  316.5 0.3 select_reduce_fusion
  316.7 140.8 %all-to-all-done.3 = bf16[64,4,6,2048]{3,1,2,0:T(4,128)(2,1)} async-done(((bf16[64,4,6,2048]{3,1,2,0:T(4,128)(2,1)}), bf16[64,4,6,2048]{3,1,2,0:T(4,128)(2,1)}, u32[]{:S(2)}, u32[]{:S(2)}) %all-to-all-start.3) | async-done | bytes 6291488 | tf_op jit(solution)/shard_map/all_to_all | solution.py:150
  457.5 10.5 %fusion.6 = bf16[4,32,2048]{2,1,0:T(8,128)(2,1)} fusion(bf16[64,4,6,2048]{3,1,2,0:T(4,128)(2,1)} %all-to-all-done.3, bf16[4,64,32]{1,2,0:T(8,128)(2,1)S(1)} %bitcast.130, s32[4,64,32]{1,2,0:T(8,128)S(1)} %subtract_bitcast_fusion, pred[4,64,32]{1,2,0:T(8,128)(4,1)S(1)} %compare_bitcast_fusion), kind=kOutput, calls=%fused_computation.10 | convolution fusion | flops 201474048 | bytes 6873088 | tf_op jit(solution)/shard_map/gxct,xgcd->gtd/dot_general | solution.py:159
  468.1 0.5 copy-done.2
  468.7 6.6 %gather_fusion.1 = s32[1024]{0:T(1024)S(1)} fusion(s32[32]{0:T(128)S(1)} %bitcast.121, s32[1024]{0:T(1024)S(1)} %bitcast_clamp_fusion), kind=kCustom, calls=%fused_computation.1 | custom fusion | bytes 12288 | tf_op jit(solution)/shard_map/jit(_take)/gather | solution.py:78
  475.3 4.0 gather_fusion.2
  479.4 1.4 copy.161
  481.6 2.6 select_select_fusion
  484.1 2.9 reduce-scatter.2.cloned.1.call-done
  487.1 1.7 fusion.39
  (67 shorter events, 1.6 us)
Async XLA Ops:
  7.2 8.4 %copy-start = (bf16[16,128,512]{2,1,0:T(8,128)(2,1)S(1)}, bf16[16,128,512]{2,1,0:T(8,128)(2,1)}, u32[]{:S(2)}) copy-start(bf16[16,128,512]{2,1,0:T(8,128)(2,1)} %param.27) | copy-start | bytes 6291460
  7.2 4.2 copy-start.4
  11.3 4.7 copy-start.9
  11.4 4.2 copy-start.11
  15.5 1.4 copy-start.5
  16.0 0.8 copy-start.6
  17.2 2.5 copy-start.15
  17.2 3.7 copy-start.3
  17.2 3.7 copy-start.7
  17.2 3.7 copy-start.10
  28.1 7.8 %copy-start.12 = (s32[4,1,32,6]{2,1,3,0:T(1,128)S(1)}, s32[4,1,32,6]{2,1,3,0:T(1,128)}, u32[]{:S(2)}) copy-start(s32[4,1,32,6]{2,1,3,0:T(1,128)} %param.31) | copy-start | bytes 9220
  31.5 20.0 %copy-start.14 = (bf16[2048]{0:T(1024)(128)(2,1)S(1)}, bf16[2048]{0:T(1024)(128)(2,1)}, u32[]{:S(2)}) copy-start(bf16[2048]{0:T(1024)(128)(2,1)} %param.30) | copy-start | bytes 12292
  31.5 13.9 %all-to-all-start = ((bf16[4,32,2048]{2,1,0:T(8,128)(2,1)}), bf16[4,32,2048]{2,1,0:T(8,128)(2,1)S(1)}, u32[]{:S(2)}, u32[]{:S(2)}) async-start(bf16[4,32,2048]{2,1,0:T(8,128)(2,1)} %tile.9), calls=%async_computation | async-start | bytes 1048576 | tf_op jit(solution)/shard_map/all_to_all | solution.py:14
  45.4 12.5 %copy-start.8 = (bf16[1,32,2048]{2,1,0:T(8,128)(2,1)S(1)}, bf16[1,32,2048]{2,1,0:T(8,128)(2,1)}, u32[]{:S(2)}) copy-start(bf16[1,32,2048]{2,1,0:T(8,128)(2,1)} %param.18) | copy-start | bytes 393220
  48.1 9.3 %all-to-all-start.1 = ((bf16[4,32,512]{2,1,0:T(8,128)(2,1)}), bf16[4,32,512]{2,1,0:T(8,128)(2,1)S(1)}, u32[]{:S(2)}, u32[]{:S(2)}) async-start(bf16[4,32,512]{2,1,0:T(8,128)(2,1)} %bitcast.15), calls=%async_computation.1 | async-start | bytes 262144 | tf_op jit(solution)/shard_map/all_to_all | solution.py:127
  310.5 5.8 %copy-start.13 = (f32[4,1,32,6]{2,1,3,0:T(1,128)S(1)}, f32[4,1,32,6]{2,1,3,0:T(1,128)}, u32[]{:S(2)}) copy-start(f32[4,1,32,6]{2,1,3,0:T(1,128)} %param.32) | copy-start | bytes 9220
  310.5 5.9 %copy-start.16 = (s32[1,8]{1,0:T(1,128)S(1)}, s32[1,8]{1,0:T(1,128)}, u32[]{:S(2)}) copy-start(s32[1,8]{1,0:T(1,128)} %param.22) | copy-start | bytes 100
  310.5 147.0 %all-to-all-start.3 = ((bf16[64,4,6,2048]{3,1,2,0:T(4,128)(2,1)}), bf16[64,4,6,2048]{3,1,2,0:T(4,128)(2,1)}, u32[]{:S(2)}, u32[]{:S(2)}) async-start(bf16[64,4,6,2048]{3,1,2,0:T(4,128)(2,1)} %copy.159), calls=%async_computation.3 | async-start | bytes 12582912 | tf_op jit(solution)/shard_map/all_to_all | solution.py:150
  316.2 170.8 %reduce-scatter.2.cloned.1.call-start = ((), (), s32[]{:S(2)}) async-start(), calls=%async_computation.5 | async-start | bytes 655360 | tf_op jit(solution)/shard_map/reduce_scatter | solution.py:160
  468.0 0.7 copy-start.2
  481.5 7.2 %copy-start.1 = (bf16[16,128,512]{2,1,0:T(8,128)(2,1)S(1)}, bf16[16,128,512]{2,1,0:T(8,128)(2,1)}, u32[]{:S(2)}) copy-start(bf16[16,128,512]{2,1,0:T(8,128)(2,1)} %param.27) | copy-start | bytes 6291460
Sparse Core Ops, SparseCore 0:
  468.2 18.8 reduce-scatter.1
